TPU v7x, 128 devices: a whole 4x4x4 slice. The times are simulated.
128 devices in a mesh: row: 32 (over x, y, core), col: 4 (over z).
Axes of the slice: x: 4, y: 4, z: 4, core: 2. Of those that a mesh axis runs over, the one named last changes fastest.
Arguments:
- frames: float32 [64, 65536], P(None, ('row', 'col')), may hold values from -8 to 8
- start: float32 [32, 65536], P(None, ('row', 'col')), may hold values from -6 to 6
Outputs:
- basis: float32 [32, 65536], P(None, ('row', 'col'))
All inputs are finite; a program needn't handle non-finite values.
Results may differ from a plain program's by a relative error of at most 0.0003.
Values sent between devices are 32-bit elements; how exact they have to be, the bound alone decides.
A program may use at most 320 MiB of HBM per device.

v0:
```python
import jax
import jax.numpy as jnp
from jax import lax
from jax.sharding import PartitionSpec as P


def build_block(block_points, block_squares, column_points, column_squares):
    products = lax.dot_general(
        block_points, column_points, (((0,), (0,)), ((), ())), precision=lax.Precision.HIGHEST
    )
    distance = block_squares[:, None] + column_squares[None, :] - 2.0 * products
    return jnp.exp(-distance / (0.5 * block_points.shape[0]))


def shards(frames, start):
    block_points = lax.all_gather(frames, "col", axis=1, tiled=True)
    column_points = lax.all_gather(frames, "row", axis=1, tiled=True)
    block_squares = jnp.sum(block_points * block_points, axis=0)
    column_squares = jnp.sum(column_points * column_points, axis=0)
    frame_count = frames.shape[1] * lax.axis_size("row") * lax.axis_size("col")
    block_rows = block_points.shape[1]
    height = min(512, block_rows)
    rounds = block_rows // height

    def kernel_part(index):
        first = index * height
        return build_block(
            block_points[:, first : first + height],
            block_squares[first : first + height],
            column_points,
            column_squares,
        )

    stored = [kernel_part(index) for index in range(rounds)]

    def fetch_tile(index):
        return stored[index]

    def sweep_kernel(spread_weights):
        pieces = []
        for index in range(rounds):
            part = fetch_tile(index)
            if spread_weights is None:
                pieces.append(jnp.sum(part, axis=1)[None, :])
            else:
                pieces.append(
                    lax.dot_general(
                        spread_weights,
                        part,
                        (((1,), (1,)), ((), ())),
                        precision=lax.Precision.HIGHEST,
                    )
                )
        result = jnp.concatenate(pieces, axis=1)
        return result

    def settle(partial_value):
        summed = lax.psum_scatter(partial_value, "col", scatter_dimension=1, tiled=True)
        return summed

    def kernel_product(weights):
        spread_weights = lax.all_gather(weights, "row", axis=1, tiled=True)
        return settle(sweep_kernel(spread_weights))

    def gram_matrix(vectors):
        local_gram = jnp.dot(vectors, vectors.T, precision=lax.Precision.HIGHEST)
        return lax.psum(local_gram, ("row", "col")) / frame_count

    def orthonormal(vectors):
        factor = jnp.linalg.cholesky(gram_matrix(vectors))
        return jax.scipy.linalg.solve_triangular(factor, vectors, lower=True)

    density = settle(sweep_kernel(None))[0]
    inverse = 1.0 / density
    scaled = start * inverse[None, :]
    degree = kernel_product(inverse[None, :])[0]
    product = kernel_product(scaled)
    grown_one = product / degree[None, :]
    basis_one = orthonormal(grown_one)
    grown_two = kernel_product(basis_one * inverse[None, :]) / degree[None, :]
    return orthonormal(grown_two)


def solution(mesh):
    return jax.shard_map(
        shards,
        mesh=mesh,
        in_specs=(P(None, ("row", "col")), P(None, ("row", "col"))),
        out_specs=P(None, ("row", "col")),
        check_vma=False,
    )
```

profile of v0, /device:TPU:1, one launch (start us, length us, event | category | flops | bytes accessed | tf_op | source)
XLA Modules:
  0.0 895.1 jit_solution(2767273097480972749)
XLA Ops:
  6.5 0.7 all-gather.4.cloned.1.call-update
  7.3 0.0 reduce-scatter.13.cloned.1.call-start
  7.3 13.6 %all_gather.15 = f32[64,2048]{1,0:T(8,128)S(1)} all-gather(f32[64,512]{1,0:T(8,128)} %param.5), channel_id=1, replica_groups=mesh['row'=32,'col'=4] {'col'}, dimensions={1}, use_global_device_ids=true | all-gather | bytes 655360 | tf_op jit(solution)/shard_map/all_gather | solution.py:16
  20.9 0.1 multiply_reduce_fusion.1
  21.0 38.4 %all-gather.4.cloned.1.call-done = f32[64,16384]{1,0:T(8,128)} async-done(((f32[64,512]{1,0:T(8,128)}), f32[64,16384]{1,0:T(8,128)}) %all-gather.4.cloned.1.call-update) | async-done | bytes 4194320 | tf_op jit(solution)/shard_map/all_gather | solution.py:17
  59.3 2.7 multiply_reduce_fusion
  62.1 37.7 %fusion.27 = (f32[512]{0:T(512)S(1)}, f32[512,16384]{1,0:T(8,128)}) fusion(f32[64,16384]{1,0:T(8,128)} %all-gather.4.cloned.1.call-done, f32[64,2048]{1,0:T(8,128)S(1)} %all_gather.15, f32[16384]{0:T(1024)S(1)} %multiply_reduce_fusion, f32[512]{0:T(512)S(1)} %get-tuple-element.6), kind=kOutput, calls=%fused_computation.53 | convolution fusion | flops 6492782080 | bytes 37949440 | tf_op jit(solution)/shard_map/dot_general | solution.py:8
  99.8 37.0 %fusion.24 = (f32[512]{0:T(512)S(1)}, f32[512,16384]{1,0:T(8,128)}) fusion(f32[64,16384]{1,0:T(8,128)S(1)} %copy-done.2, f32[64,2048]{1,0:T(8,128)S(1)} %all_gather.15, f32[16384]{0:T(1024)S(1)} %multiply_reduce_fusion, f32[512]{0:T(512)S(1)} %get-tuple-element.8), kind=kOutput, calls=%fused_computation.50 | convolution fusion | flops 6492782080 | bytes 37949440 | tf_op jit(solution)/shard_map/dot_general | solution.py:8
  136.8 36.6 %fusion.25 = (f32[512]{0:T(512)S(1)}, f32[512,16384]{1,0:T(8,128)}) fusion(f32[64,16384]{1,0:T(8,128)S(1)} %copy-done.2, f32[64,2048]{1,0:T(8,128)S(1)} %all_gather.15, f32[16384]{0:T(1024)S(1)} %multiply_reduce_fusion, f32[512]{0:T(512)S(1)} %get-tuple-element.9), kind=kOutput, calls=%fused_computation.51 | convolution fusion | flops 6492782080 | bytes 37949440 | tf_op jit(solution)/shard_map/dot_general | solution.py:8
  173.4 36.7 %fusion.26 = (f32[512]{0:T(512)S(1)}, f32[512,16384]{1,0:T(8,128)}) fusion(f32[64,16384]{1,0:T(8,128)S(1)} %copy-done.2, f32[64,2048]{1,0:T(8,128)S(1)} %all_gather.15, f32[16384]{0:T(1024)S(1)} %multiply_reduce_fusion, f32[512]{0:T(512)S(1)} %get-tuple-element.10), kind=kOutput, calls=%fused_computation.52 | convolution fusion | flops 6492782080 | bytes 37949440 | tf_op jit(solution)/shard_map/dot_general | solution.py:8
  210.1 1.4 copy.13
  211.5 0.0 reduce-scatter.13.cloned.1.call-update
  211.5 0.0 all-gather.6.cloned.1.call-start
  211.6 21.5 %reduce-scatter.13.cloned.1.call-done = f32[512,1]{1,0:T(8,128)} async-done(((f32[2048,1]{1,0:T(8,128)}), f32[512,1]{1,0:T(8,128)}) %reduce-scatter.13.cloned.1.call-update) | async-done | bytes 2064
  233.0 1.1 copy.14
  234.1 26.0 %all_gather.18 = f32[1,16384]{1,0:T(1,128)S(1)} all-gather(f32[1,512]{1,0:T(1,128)S(1)} %broadcast_divide_fusion.6), channel_id=1, replica_groups=mesh['row'=32,'col'=4] {'row'}, dimensions={1}, use_global_device_ids=true | all-gather | bytes 67584 | tf_op jit(solution)/shard_map/all_gather | solution.py:62
  260.1 0.6 broadcast_multiply_fusion
  260.7 0.0 all-gather.6.cloned.1.call-update
  260.8 0.0 reduce-scatter.15.cloned.1.call-start
  260.8 31.2 %fusion.8 = f32[1,512]{1,0:T(1,128)S(1)} fusion(f32[512,16384]{1,0:T(8,128)} %get-tuple-element.16, f32[1,16384]{1,0:T(1,128)S(1)} %all_gather.18), kind=kOutput, calls=%fused_computation.17 | convolution fusion | flops 100663296 | bytes 33622016 | tf_op jit(solution)/shard_map/dot_general | solution.py:47
  292.0 30.9 %fusion.6 = f32[1,512]{1,0:T(1,128)S(1)} fusion(f32[512,16384]{1,0:T(8,128)} %get-tuple-element.14, f32[1,16384]{1,0:T(1,128)S(1)} %all_gather.18), kind=kOutput, calls=%fused_computation.15 | convolution fusion | flops 100663296 | bytes 33622016 | tf_op jit(solution)/shard_map/dot_general | solution.py:47
  322.9 31.0 %fusion.4 = f32[1,512]{1,0:T(1,128)S(1)} fusion(f32[512,16384]{1,0:T(8,128)} %get-tuple-element.12, f32[1,16384]{1,0:T(1,128)S(1)} %all_gather.18), kind=kOutput, calls=%fused_computation.13 | convolution fusion | flops 100663296 | bytes 33622016 | tf_op jit(solution)/shard_map/dot_general | solution.py:47
  353.9 30.8 %fusion.10 = f32[1,512]{1,0:T(1,128)S(1)} fusion(f32[512,16384]{1,0:T(8,128)} %get-tuple-element.18, f32[1,16384]{1,0:T(1,128)S(1)} %all_gather.18), kind=kOutput, calls=%fused_computation.19 | convolution fusion | flops 100663296 | bytes 33622016 | tf_op jit(solution)/shard_map/dot_general | solution.py:47
  384.7 1.4 copy.15
  386.0 0.0 reduce-scatter.15.cloned.1.call-update
  386.1 0.0 reduce-scatter.9.cloned.1.call-start
  386.1 0.0 all-gather.6.cloned.1.call-done
  386.2 34.4 %fusion.31 = f32[32,512]{1,0:T(8,128)S(1)} fusion(f32[32,16384]{1,0:T(8,128)} %all-gather.6.cloned.1.call-done, f32[512,16384]{1,0:T(8,128)} %get-tuple-element.12), kind=kOutput, calls=%fused_computation.57 | convolution fusion | flops 3221225472 | bytes 35717120 | tf_op jit(solution)/shard_map/dot_general | solution.py:47
  420.5 33.9 %fusion.30 = f32[32,512]{1,0:T(8,128)S(1)} fusion(f32[32,16384]{1,0:T(8,128)S(1)} %copy-done, f32[512,16384]{1,0:T(8,128)} %get-tuple-element.14), kind=kOutput, calls=%fused_computation.56 | convolution fusion | flops 3221225472 | bytes 35717120 | tf_op jit(solution)/shard_map/dot_general | solution.py:47
  454.4 34.3 %fusion.29 = f32[32,512]{1,0:T(8,128)S(1)} fusion(f32[32,16384]{1,0:T(8,128)S(1)} %copy-done, f32[512,16384]{1,0:T(8,128)} %get-tuple-element.16), kind=kOutput, calls=%fused_computation.55 | convolution fusion | flops 3221225472 | bytes 35717120 | tf_op jit(solution)/shard_map/dot_general | solution.py:47
  488.8 33.9 %fusion.28 = f32[32,512]{1,0:T(8,128)S(1)} fusion(f32[32,16384]{1,0:T(8,128)S(1)} %copy-done, f32[512,16384]{1,0:T(8,128)} %get-tuple-element.18), kind=kOutput, calls=%fused_computation.54 | convolution fusion | flops 3221225472 | bytes 35717120 | tf_op jit(solution)/shard_map/dot_general | solution.py:47
  522.6 0.7 pad_maximum_fusion
  523.3 0.0 reduce-scatter.9.cloned.1.call-update
  523.4 0.0 all-gather.8.cloned.1.call-start
  523.4 0.0 reduce-scatter.15.cloned.1.call-done
  523.4 1.1 copy.16
  524.5 14.8 %reduce-scatter.9.cloned.1.call-done = f32[32,512]{1,0:T(8,128)} async-done(((f32[32,2048]{1,0:T(8,128)}), f32[32,512]{1,0:T(8,128)}) %reduce-scatter.9.cloned.1.call-update) | async-done | bytes 65552 | tf_op jit(solution)/shard_map/reduce_scatter | solution.py:58
  539.3 1.1 fusion.12
  540.4 67.2 %psum.14 = f32[32,32]{0,1:T(8,128)S(1)} all-reduce(f32[32,32]{0,1:T(8,128)S(1)} %fusion.12), channel_id=1, replica_groups=mesh['row'=32,'col'=4] {'row','col'}, use_global_device_ids=true, to_apply=%region_9.0 | all-reduce | flops 1024 | bytes 8192 | tf_op jit(solution)/shard_map/psum | solution.py:67
  607.6 0.1 copy.8
  607.7 2.9 cholesky.44
  610.6 0.6 compare_reduce_fusion.1
  611.3 0.7 fusion.15
  611.9 2.4 custom-call.6
  614.4 1.8 convolution_multiply_fusion
  616.1 0.0 all-gather.8.cloned.1.call-update
  616.1 0.0 reduce-scatter.11.cloned.1.call-start
  616.2 40.7 %all-gather.8.cloned.1.call-done = f32[32,16384]{1,0:T(8,128)} async-done(((f32[32,512]{1,0:T(8,128)}), f32[32,16384]{1,0:T(8,128)}) %all-gather.8.cloned.1.call-update) | async-done | bytes 2097168 | tf_op jit(solution)/shard_map/all_gather | solution.py:62
  656.8 34.2 %fusion.35 = f32[32,512]{1,0:T(8,128)S(1)} fusion(f32[32,16384]{1,0:T(8,128)} %all-gather.8.cloned.1.call-done, f32[512,16384]{1,0:T(8,128)} %get-tuple-element.12), kind=kOutput, calls=%fused_computation.61 | convolution fusion | flops 3221225472 | bytes 35717120 | tf_op jit(solution)/shard_map/dot_general | solution.py:47
  691.0 0.0 copy-done.1
  691.0 33.9 %fusion.34 = f32[32,512]{1,0:T(8,128)S(1)} fusion(f32[32,16384]{1,0:T(8,128)S(1)} %copy-done.1, f32[512,16384]{1,0:T(8,128)} %get-tuple-element.14), kind=kOutput, calls=%fused_computation.60 | convolution fusion | flops 3221225472 | bytes 35717120 | tf_op jit(solution)/shard_map/dot_general | solution.py:47
  724.9 34.1 %fusion.33 = f32[32,512]{1,0:T(8,128)S(1)} fusion(f32[32,16384]{1,0:T(8,128)S(1)} %copy-done.1, f32[512,16384]{1,0:T(8,128)} %get-tuple-element.16), kind=kOutput, calls=%fused_computation.59 | convolution fusion | flops 3221225472 | bytes 35717120 | tf_op jit(solution)/shard_map/dot_general | solution.py:47
  759.0 33.9 %fusion.32 = f32[32,512]{1,0:T(8,128)S(1)} fusion(f32[32,16384]{1,0:T(8,128)S(1)} %copy-done.1, f32[512,16384]{1,0:T(8,128)} %get-tuple-element.18), kind=kOutput, calls=%fused_computation.58 | convolution fusion | flops 3221225472 | bytes 35717120 | tf_op jit(solution)/shard_map/dot_general | solution.py:47
  792.9 0.7 pad_maximum_fusion.1
  793.6 0.0 reduce-scatter.11.cloned.1.call-update
  793.6 17.6 %reduce-scatter.11.cloned.1.call-done = f32[32,512]{1,0:T(8,128)} async-done(((f32[32,2048]{1,0:T(8,128)}), f32[32,512]{1,0:T(8,128)}) %reduce-scatter.11.cloned.1.call-update) | async-done | bytes 65552 | tf_op jit(solution)/shard_map/reduce_scatter | solution.py:58
  811.2 1.1 fusion.14
  812.3 67.0 %psum.15 = f32[32,32]{0,1:T(8,128)S(1)} all-reduce(f32[32,32]{0,1:T(8,128)S(1)} %fusion.14), channel_id=1, replica_groups=mesh['row'=32,'col'=4] {'row','col'}, use_global_device_ids=true, to_apply=%region_13.16 | all-reduce | flops 1024 | bytes 8192 | tf_op jit(solution)/shard_map/psum | solution.py:67
  879.3 0.1 copy.10
  879.4 2.9 cholesky.55
  882.4 0.6 compare_reduce_fusion
  883.0 0.7 fusion.16
  883.7 2.4 custom-call.7
  886.1 1.8 fusion.13
  (18 shorter events, 0.1 us)
Async XLA Ops:
  6.5 52.8 %all-gather.4.cloned.1.call-start = ((), (), s32[]{:S(2)}) async-start(), calls=%async_computation.4 | async-start | bytes 4325376 | tf_op jit(solution)/shard_map/all_gather | solution.py:17
  7.3 225.8 %reduce-scatter.13.cloned.1.call-start = ((), (), s32[]{:S(2)}) async-start(), calls=%async_computation.9 | async-start | bytes 1310720
  59.3 40.5 %copy-start.2 = (f32[64,16384]{1,0:T(8,128)S(1)}, f32[64,16384]{1,0:T(8,128)}, u32[]{:S(2)}) copy-start(f32[64,16384]{1,0:T(8,128)} %all-gather.4.cloned.1.call-done) | copy-start | bytes 12582916
  173.4 86.7 %copy-start.3 = (f32[32,512]{1,0:T(8,128)S(1)}, f32[32,512]{1,0:T(8,128)}, u32[]{:S(2)}) copy-start(f32[32,512]{1,0:T(8,128)} %param.6) | copy-start | bytes 196612
  211.5 174.6 %all-gather.6.cloned.1.call-start = ((), (), s32[]{:S(2)}) async-start(), calls=%async_computation.5 | async-start | bytes 2162688 | tf_op jit(solution)/shard_map/all_gather | solution.py:62
  260.8 262.7 %reduce-scatter.15.cloned.1.call-start = ((), (), s32[]{:S(2)}) async-start(), calls=%async_computation.10 | async-start | bytes 1310720
  386.1 153.2 %reduce-scatter.9.cloned.1.call-start = ((), (), s32[]{:S(2)}) async-start(), calls=%async_computation.6 | async-start | bytes 327680 | tf_op jit(solution)/shard_map/reduce_scatter | solution.py:58
  386.1 34.4 %copy-start = (f32[32,16384]{1,0:T(8,128)S(1)}, f32[32,16384]{1,0:T(8,128)}, u32[]{:S(2)}) copy-start(f32[32,16384]{1,0:T(8,128)} %all-gather.6.cloned.1.call-done) | copy-start | bytes 6291460
  523.4 133.5 %all-gather.8.cloned.1.call-start = ((), (), s32[]{:S(2)}) async-start(), calls=%async_computation.7 | async-start | bytes 2162688 | tf_op jit(solution)/shard_map/all_gather | solution.py:62
  616.1 195.1 %reduce-scatter.11.cloned.1.call-start = ((), (), s32[]{:S(2)}) async-start(), calls=%async_computation.8 | async-start | bytes 327680 | tf_op jit(solution)/shard_map/reduce_scatter | solution.py:58
  656.8 34.2 %copy-start.1 = (f32[32,16384]{1,0:T(8,128)S(1)}, f32[32,16384]{1,0:T(8,128)}, u32[]{:S(2)}) copy-start(f32[32,16384]{1,0:T(8,128)} %all-gather.8.cloned.1.call-done) | copy-start | bytes 6291460
Sparse Core Ops, SparseCore 0:
  9.7 49.5 all-gather.3
  211.6 21.3 reduce-scatter.12
  260.9 41.3 all-gather.5
  386.2 19.1 reduce-scatter.14
  523.5 15.7 reduce-scatter.8
  616.3 40.5 all-gather.7
  793.7 17.4 reduce-scatter.10
where the time goes:
time: 902 us; the launch traced here: 895 us
  matrix products  550 us (61%)
  blocking collectives  174 us (19%)
  waiting for transfers between devices  134 us (15%)
  other arithmetic  18.3 us (2%)
  between operations  14 us (2%)
    dot_general x12, matrix products, sweep_kernel(): lax.dot_general(spread_weights, part, (((1,), (1,)), ((), ())), precision...  396 us
    dot_general x4, matrix products, build_block(): lax.dot_general(block_points, column_points, (((0,), (0,)), ((), ())), pr...  148 us
    psum x2, blocking collectives, gram_matrix(): return lax.psum(local_gram, ('row', 'col')) / frame_count  134 us
    all_gather x2, waiting for transfers between devices, kernel_product(): spread_weights = lax.all_gather(weights, 'row', axis=1, tiled=True)  40.7 us
    all_gather x1, waiting for transfers between devices, shards(): column_points = lax.all_gather(frames, 'row', axis=1, tiled=True)  38.4 us
    reduce_scatter x2, waiting for transfers between devices, settle(): lax.psum_scatter(partial_value, 'col', scatter_dimension=1, tiled=True)  32.4 us
    all_gather x1, blocking collectives, kernel_product(): spread_weights = lax.all_gather(weights, 'row', axis=1, tiled=True)  26 us
    unnamed x9, waiting for transfers between devices  22.3 us
  transfers between devices with their start and end apart: 7, of which 5 were waited for; matrix products, arithmetic and copies ran while one was open for 29% of the time, Pallas kernels for 0%

commit v1 on v0

v1 whole, which is shorter than its diff:
```python
import math

import jax
import jax.numpy as jnp
from jax import lax
from jax.experimental import pallas as pl
from jax.experimental.pallas import tpu as pltpu
from jax.sharding import PartitionSpec as P

MESH = pl.DeviceIdType.MESH
BF = jnp.bfloat16
F8 = jnp.float8_e4m3fn
F32 = jnp.float32
LOW_SCALE = 2.0**17
STAGES = 3
KEPT = (2, 4, 6)
SENT = (0, 1, 3, 5, 7)


def features(points, stationary):
    scaled = points * math.sqrt(math.log2(math.e) / 16.0 * (64.0 / points.shape[0]))
    high = scaled.astype(BF)
    low = (scaled - high.astype(F32)).astype(BF)
    half = 0.5 * jnp.sum(scaled * scaled, axis=0, keepdims=True)
    one = half.astype(BF).astype(F32)
    two = (half - one).astype(BF).astype(F32)
    three = half - one - two
    row = lax.broadcasted_iota(jnp.int32, (16, points.shape[1]), 0)
    unit = jnp.ones_like(one)
    if stationary:
        first, rest, middle = (-one, -two, -three), (-unit, -unit, -unit), (high, high, low)
    else:
        first, rest, middle = (unit, unit, unit), (one, two, three), (high, low, high)
    extra = jnp.zeros((16, points.shape[1]), F32)
    for index, value in enumerate(first + rest):
        extra = jnp.where(row == index, value, extra)
    pad = jnp.zeros((48, points.shape[1]), BF)
    return jnp.concatenate(middle + (extra.astype(BF), pad), axis=0)


def inverse_factor(gram):
    n = gram.shape[0]
    row = lax.broadcasted_iota(jnp.int32, (n, n), 0)
    column = lax.broadcasted_iota(jnp.int32, (n, n), 1)
    inverse = jnp.where(row == column, 1.0, 0.0).astype(F32)
    for c in range(n):
        pivot = gram[c : c + 1, c : c + 1]
        root = lax.rsqrt(pivot)
        root = root * (1.5 - 0.5 * pivot * root * root)
        line = gram[c : c + 1, :] * root
        line_inverse = inverse[c : c + 1, :] * root
        factor = jnp.where(row[:, :1] > c, gram[:, c : c + 1] * root, 0.0)
        gram = jnp.where(row == c, line, gram - factor * line)
        inverse = jnp.where(row == c, line_inverse, inverse - factor * line_inverse)
    return inverse


def kernel(
    X, Z, frames, start, out, far_high, far_low,
    near_high, near_low, stage_high, stage_low, zframes, fall, sall, gall, iall, stat, turned,
    acc, low_acc, dacc, part, dgot, got_one, got_two, degree, gram_part, gram_all, gram_sum, gram_col, ready,
    f_recv, s_recv, g_recv, zf_recv, d_recv, i_recv, one_recv, two_recv, p_recv, q_recv,
    send, forward, write_sem, read_sem,
):
    NO = X * X
    NB = 2 * NO
    B = frames.shape[1]
    R = Z * B
    V = start.shape[0]
    NH = len(SENT) * (NB // 8)
    total = X * X * 2 * Z * B
    me, z = lax.axis_index("row"), lax.axis_index("col")
    core, chip = lax.rem(me, 2), me // 2
    cx, cy = chip // X, lax.rem(chip, X)

    def plane(o):
        return {"row": (lax.rem(cx + o // X, X) * X + lax.rem(cy + lax.rem(o, X), X)) * 2 + core, "col": z}

    def back(o):
        return lax.rem(X - o // X, X) * X + lax.rem(X - lax.rem(o, X), X)

    sibling = {"row": chip * 2 + 1 - core, "col": z}

    def along(dz):
        return {"row": me, "col": lax.rem(z + dz, Z)}

    def post(d):
        return {"row": chip * 2 + lax.rem(core + d // Z, 2), "col": lax.rem(z + lax.rem(d, Z), Z)}

    def post_back(d):
        return (d // Z) * Z + lax.rem(Z - lax.rem(d, Z), Z)

    def push(src, dst, send_sem, recv_sem, device):
        pltpu.make_async_remote_copy(
            src_ref=src, dst_ref=dst, send_sem=send_sem, recv_sem=recv_sem, device_id=device, device_id_type=MESH
        ).start()

    def arrived(ref, sem):
        pltpu.make_async_remote_copy(
            src_ref=ref, dst_ref=ref, send_sem=send.at[0], recv_sem=sem, device_id=sibling, device_id_type=MESH
        ).wait_recv()

    def left(ref, sem):
        pltpu.make_async_remote_copy(
            src_ref=ref, dst_ref=ref, send_sem=sem, recv_sem=f_recv.at[0], device_id=sibling, device_id_type=MESH
        ).wait_send()

    def gather_start(mine, buffer, recv, sem, forward_sem):
        push(mine, buffer.at[1], forward_sem, recv.at[1], sibling)

        def each(o, _):
            slot = 2 * back(o)
            push(mine, buffer.at[slot], sem, recv.at[slot], plane(o))
            return 0

        lax.fori_loop(1, NO, each, 0)

    def pass_on(o, buffer, recv, forward_sem):
        arrived(buffer.at[2 * o], recv.at[2 * o])
        push(buffer.at[2 * o], buffer.at[2 * o + 1], forward_sem, recv.at[2 * o + 1], sibling)

    def gather_end(buffer, sem, forward_sem):
        left(buffer.at[pl.ds(0, NO - 1)], sem)
        left(buffer.at[pl.ds(0, NO)], forward_sem)

    def col_sum_start(source, target, recv, sem):
        for dz in range(1, Z):
            push(source.at[dz], target.at[Z - dz], sem, recv.at[Z - dz], along(dz))

    barrier = pltpu.get_barrier_semaphore()

    def greet_plane(o, _):
        pl.semaphore_signal(barrier, inc=1, device_id=plane(o), device_id_type=MESH)
        return 0

    def greet_post(d, _):
        pl.semaphore_signal(barrier, inc=1, device_id=post(d), device_id_type=MESH)
        return 0

    lax.fori_loop(1, NO, greet_plane, 0)
    lax.fori_loop(1, 2 * Z, greet_post, 0)
    pl.semaphore_wait(barrier, NO - 1 + 2 * Z - 1)

    for dz in range(1, Z):
        push(frames, zframes.at[Z - dz], send.at[1], zf_recv.at[Z - dz], along(dz))
    gather_start(frames, fall, f_recv, send.at[0], forward.at[0])
    gather_start(start, sall, s_recv, send.at[2], forward.at[1])
    fall[0] = frames[...]
    sall[0] = start[...]
    dacc[...] = jnp.zeros_like(dacc)
    stat[:, 0:B] = features(frames[...], True)
    for dz in range(1, Z):
        arrived(zframes.at[dz], zf_recv.at[dz])
        stat[:, dz * B : (dz + 1) * B] = features(zframes[dz], True)

    def writes(h):
        slot = lax.rem(h, STAGES)
        return (
            pltpu.make_async_copy(stage_high.at[slot], far_high.at[h], write_sem.at[slot, 0]),
            pltpu.make_async_copy(stage_low.at[slot], far_low.at[h], write_sem.at[slot, 1]),
        )

    def reads(h):
        slot = lax.rem(h, STAGES)
        return (
            pltpu.make_async_copy(far_high.at[h], stage_high.at[slot], read_sem.at[slot, 0]),
            pltpu.make_async_copy(far_low.at[h], stage_low.at[slot], read_sem.at[slot, 1]),
        )

    width = min(512, R)

    def build(n, high_ref, low_ref):
        turned[...] = features(fall[n], False).T
        for c in range(R // width):
            at = slice(c * width, (c + 1) * width)
            power = jnp.dot(turned[...], stat[:, at], preferred_element_type=F32)
            value = jnp.exp2(power)
            high = value.astype(BF)
            high_ref[:, at] = high
            low_ref[:, at] = ((value - high.astype(F32)) * LOW_SCALE).astype(F8)
            dacc[:, at] += jnp.sum(value.reshape(B // 8, 8, width), axis=0)

    def build_group(g, _):
        for i in range(8):
            n = g * 8 + i
            if i % 2 == 0:
                o = g * 4 + i // 2

                @pl.when(o + 1 < NO)
                def _():
                    pass_on(o + 1, fall, f_recv, forward.at[0])
            else:
                arrived(fall.at[n], f_recv.at[n])
            if i in KEPT:
                at = g * len(KEPT) + KEPT.index(i)
                build(n, near_high.at[at], near_low.at[at])
            else:
                h = g * len(SENT) + SENT.index(i)

                @pl.when(h >= STAGES)
                def _():
                    for copy in writes(h - STAGES):
                        copy.wait()

                slot = lax.rem(h, STAGES)
                build(n, stage_high.at[slot], stage_low.at[slot])
                for copy in writes(h):
                    copy.start()
        return 0

    lax.fori_loop(0, NB // 8, build_group, 0)

    for dz in range(Z):
        part[dz, 0:8, :] = dacc[:, dz * B : (dz + 1) * B]
    for dz in range(1, Z):
        push(part.at[dz, pl.ds(0, 8)], dgot.at[Z - dz], send.at[3], d_recv.at[Z - dz], along(dz))
    for h in range(NH - STAGES, NH):
        for copy in writes(h):
            copy.wait()
    for h in range(STAGES):
        for copy in reads(h):
            copy.start()

    def pass_start(o, _):
        pass_on(o, sall, s_recv, forward.at[1])
        return 0

    lax.fori_loop(1, NO, pass_start, 0)
    dgot[0] = part[0, 0:8, :]
    for dz in range(1, Z):
        arrived(dgot.at[dz], d_recv.at[dz])
    density = jnp.sum(dgot[0] + dgot[1] if Z == 2 else dgot[0] + dgot[1] + dgot[2] + dgot[3], axis=0, keepdims=True)
    iall[0] = jnp.broadcast_to(1.0 / density, (8, B))
    push(iall.at[0], iall.at[1], forward.at[2], i_recv.at[0], sibling)
    arrived(iall.at[1], i_recv.at[0])

    def send_inverse(o, _):
        slot = back(o)
        push(iall.at[pl.ds(0, 2)], iall.at[pl.ds(2 * slot, 2)], send.at[4], i_recv.at[slot], plane(o))
        return 0

    lax.fori_loop(1, NO, send_inverse, 0)
    acc[...] = jnp.zeros_like(acc)
    low_acc[...] = jnp.zeros_like(low_acc)
    gather_end(fall, send.at[0], forward.at[0])
    gather_end(sall, send.at[2], forward.at[1])
    left(zframes.at[pl.ds(0, Z - 1)], send.at[1])
    left(dgot.at[pl.ds(0, Z - 1)], send.at[3])

    def take_inverse(o, _):
        arrived(iall.at[pl.ds(2 * o, 2)], i_recv.at[o])
        return 0

    lax.fori_loop(1, NO, take_inverse, 0)
    largest = jnp.max(jnp.max(jnp.max(iall[...], axis=0), axis=0, keepdims=True), axis=1, keepdims=True)
    low_weight = 400.0 / (6.0 * largest)

    def sweep(n, vectors, with_degree, high_ref, low_ref):
        inverse = iall[n]
        weights = vectors[n] * inverse[0:1, :]
        high = weights.astype(BF)
        low = (weights - high.astype(F32)).astype(BF)
        rows = 2 * V
        pieces = [high, low]
        if with_degree:
            inverse_high = inverse.astype(BF)
            pieces += [jnp.concatenate([inverse_high.astype(F32), inverse - inverse_high.astype(F32)], axis=0).astype(BF)]
            rows += 16
        spread = jnp.concatenate(pieces, axis=0)
        acc[0:rows, :] += jnp.dot(spread, high_ref[...], preferred_element_type=F32)
        low_acc[...] += jnp.dot((weights * low_weight).astype(F8), low_ref[...], preferred_element_type=F32)

    def sweep_group(vectors, recv, with_degree, last, g, _):
        for i in range(8):
            n = g * 8 + i
            if i % 2 == 1:
                arrived(vectors.at[n], recv.at[n])
            elif last:
                o = g * 4 + i // 2

                @pl.when(o + 1 < NO)
                def _():
                    pass_on(o + 1, vectors, recv, forward.at[3])

            if i in KEPT:
                at = g * len(KEPT) + KEPT.index(i)
                sweep(n, vectors, with_degree, near_high.at[at], near_low.at[at])
            else:
                h = g * len(SENT) + SENT.index(i)
                for copy in reads(h):
                    copy.wait()
                slot = lax.rem(h, STAGES)
                sweep(n, vectors, with_degree, stage_high.at[slot], stage_low.at[slot])

                @pl.when(h + STAGES < NH)
                def _():
                    for copy in reads(h + STAGES):
                        copy.start()

        return 0

    def own_sum(got, recv, sem, with_degree):
        for dz in range(Z):
            at = slice(dz * B, (dz + 1) * B)
            part[dz, 0:V, :] = acc[0:V, at] + acc[V : 2 * V, at] + low_acc[:, at] * (1.0 / (low_weight * LOW_SCALE))
            if with_degree:
                part[dz, V : V + 8, :] = acc[2 * V : 2 * V + 8, at] + acc[2 * V + 8 : 2 * V + 16, at]
        col_sum_start(part, got, recv, sem)

    def own_total(got, recv):
        result = part[0]
        for dz in range(1, Z):
            arrived(got.at[dz], recv.at[dz])
            result = result + got[dz]
        return result

    def gram_of(vectors):
        return lax.dot_general(
            vectors, vectors, (((1,), (1,)), ((), ())), precision=lax.Precision.HIGHEST, preferred_element_type=F32
        ) * (1.0 / total)

    def gram_send(which, vectors):
        gram_all[which, 0] = gram_of(vectors)

        def each(o, _):
            slot = back(o)
            push(gram_all.at[which, 0], gram_all.at[which, slot], send.at[5 + which], p_recv.at[which, slot], plane(o))
            return 0

        lax.fori_loop(1, NO, each, 0)

    def gram_turn(which):
        def each(o, _):
            arrived(gram_all.at[which, o], p_recv.at[which, o])
            return 0

        lax.fori_loop(1, NO, each, 0)
        gram_col[which, 0] = jnp.sum(gram_all[which], axis=0)

        def out_to(d, _):
            slot = post_back(d)
            push(gram_col.at[which, 0], gram_col.at[which, slot], send.at[7 + which], q_recv.at[which, slot], post(d))
            return 0

        lax.fori_loop(1, 2 * Z, out_to, 0)

    def gram_total(which):
        def each(d, _):
            arrived(gram_col.at[which, d], q_recv.at[which, d])
            return 0

        lax.fori_loop(1, 2 * Z, each, 0)
        return jnp.sum(gram_col[which], axis=0)

    def gram_end(which):
        left(gram_all.at[which, pl.ds(0, NO - 1)], send.at[5 + which])
        left(gram_col.at[which, pl.ds(0, 2 * Z - 1)], send.at[7 + which])

    lax.fori_loop(0, NB // 8, lambda g, c: sweep_group(sall, s_recv, True, False, g, c), 0)
    for h in range(STAGES):
        for copy in reads(h):
            copy.start()
    own_sum(got_one, one_recv, send.at[9], True)
    acc[...] = jnp.zeros_like(acc)
    low_acc[...] = jnp.zeros_like(low_acc)
    left(iall.at[0], forward.at[2])
    left(iall.at[pl.ds(0, 2 * (NO - 1))], send.at[4])
    result = own_total(got_one, one_recv)
    degree[...] = result[V : V + 8, :]
    grown = result[0:V, :] / degree[0:1, :]
    gall[0] = grown
    gather_start(gall.at[0], gall, g_recv, send.at[10], forward.at[3])
    gram_send(0, grown)
    left(part.at[pl.ds(0, Z - 1)], send.at[9])

    def second_group(g, c):
        @pl.when(g == NB // 8 - 1)
        def _():
            gram_turn(0)

        return sweep_group(gall, g_recv, False, True, g, c)

    lax.fori_loop(0, NB // 8, second_group, 0)
    own_sum(got_two, two_recv, send.at[11], False)
    first = inverse_factor(gram_total(0))
    result = own_total(got_two, two_recv)
    grown_two = result[0:V, :] / degree[0:1, :]
    grown_two = jnp.dot(first, grown_two, precision=lax.Precision.HIGHEST, preferred_element_type=F32)
    gram_send(1, grown_two)
    gather_end(gall, send.at[10], forward.at[3])
    left(part.at[pl.ds(0, Z - 1)], send.at[11])
    gram_end(0)
    gram_turn(1)
    second = inverse_factor(gram_total(1))
    out[...] = jnp.dot(second, grown_two, precision=lax.Precision.HIGHEST, preferred_element_type=F32)
    gram_end(1)


def solution(mesh):
    X = math.isqrt(mesh.shape["row"] // 2)
    Z = mesh.shape["col"]
    NO, NB = X * X, 2 * X * X

    def step(frames, start):
        F, B = frames.shape
        V = start.shape[0]
        R = Z * B
        near, far = len(KEPT) * (NB // 8), len(SENT) * (NB // 8)
        vmem = pl.BlockSpec(memory_space=pltpu.VMEM)
        hbm = pl.BlockSpec(memory_space=pltpu.HBM)
        dma = pltpu.SemaphoreType.DMA
        basis, _, _ = pl.pallas_call(
            lambda *refs: kernel(X, Z, *refs),
            out_shape=(
                jax.ShapeDtypeStruct((V, B), F32),
                jax.ShapeDtypeStruct((far, B, R), BF),
                jax.ShapeDtypeStruct((far, B, R), F8),
            ),
            in_specs=[vmem, vmem],
            out_specs=(vmem, hbm, hbm),
            scratch_shapes=[
                pltpu.VMEM((near, B, R), BF),
                pltpu.VMEM((near, B, R), F8),
                pltpu.VMEM((STAGES, B, R), BF),
                pltpu.VMEM((STAGES, B, R), F8),
                pltpu.VMEM((Z, F, B), F32),
                pltpu.VMEM((NB, F, B), F32),
                pltpu.VMEM((NB, V, B), F32),
                pltpu.VMEM((NB, V, B), F32),
                pltpu.VMEM((NB, 8, B), F32),
                pltpu.VMEM((256, R), BF),
                pltpu.VMEM((B, 256), BF),
                pltpu.VMEM((2 * V + 16, R), F32),
                pltpu.VMEM((V, R), F32),
                pltpu.VMEM((8, R), F32),
                pltpu.VMEM((Z, V + 8, B), F32),
                pltpu.VMEM((Z, 8, B), F32),
                pltpu.VMEM((Z, V + 8, B), F32),
                pltpu.VMEM((Z, V + 8, B), F32),
                pltpu.VMEM((8, B), F32),
                pltpu.VMEM((V, V), F32),
                pltpu.VMEM((2, NO, V, V), F32),
                pltpu.VMEM((V, V), F32),
                pltpu.VMEM((2, 2 * Z, V, V), F32),
                pltpu.VMEM((V, V), F32),
                dma((NB,)), dma((NB,)), dma((NB,)),
                dma((Z,)), dma((Z,)), dma((NO,)), dma((Z,)), dma((Z,)),
                dma((2, NO)), dma((2, 2 * Z)),
                dma((12,)), dma((4,)), dma((STAGES, 2)), dma((STAGES, 2)),
            ],
            compiler_params=pltpu.CompilerParams(
                collective_id=0, has_side_effects=True, vmem_limit_bytes=64 * 1024 * 1024 - 512 * 1024
            ),
            name="diffusion",
        )(frames, start)
        return basis

    return jax.shard_map(
        step,
        mesh=mesh,
        in_specs=(P(None, ("row", "col")), P(None, ("row", "col"))),
        out_specs=P(None, ("row", "col")),
        check_vma=False,
    )
```

time: 902 us -> 175 us (0.19)
  matrix products: 550 us -> 0 us
  Pallas kernels: 0 us -> 174 us
  blocking collectives: 174 us -> 0 us
  waiting for transfers between devices: 134 us -> 0 us
  other arithmetic: 18.3 us -> 0 us
  between operations: 14 us -> 0.01 us
    dot_general x18 -> x0, matrix products: 547 us -> none  [the longest x12 396 us: sweep_kernel(): lax.dot_general(spread_weights, part, (((1,), (1,)), ((), ())), precision...]
    pallas_call x0 -> x1, Pallas kernels: none -> 174 us  [step(): pl.pallas_call(lambda *refs: kernel(X, Z, *refs), out_shape=(jax.ShapeDty...]
    psum x2 -> x0, blocking collectives: 134 us -> none  [gram_matrix(): return lax.psum(local_gram, ('row', 'col')) / frame_count]
    all_gather x3 -> x0, waiting for transfers between devices: 79 us -> none  [the longest x2 40.7 us: kernel_product(): spread_weights = lax.all_gather(weights, 'row', axis=1, tiled=True)]
    all_gather x2 -> x0, blocking collectives: 39.6 us -> none  [the longest x1 26 us: kernel_product(): spread_weights = lax.all_gather(weights, 'row', axis=1, tiled=True)]
    reduce_scatter x2 -> x0, waiting for transfers between devices: 32.4 us -> none  [settle(): lax.psum_scatter(partial_value, 'col', scatter_dimension=1, tiled=True)]
    unnamed x9 -> x0, waiting for transfers between devices: 22.3 us -> none
    another operation x10 -> x0, other arithmetic: 13.4 us -> none  [the longest x6 7.19 us: orthonormal(): factor = jnp.linalg.cholesky(gram_matrix(vectors))]
  transfers between devices with their start and end apart: 7 -> 0, of which waited for: 5 -> 0; matrix products, arithmetic and copies ran while one was open for 29% -> 0% of each run, Pallas kernels for 0% -> 0%
where the time goes in v1:
time: 175 us
  Pallas kernels  174 us (99%)
    pallas_call x1, Pallas kernels, step(): pl.pallas_call(lambda *refs: kernel(X, Z, *refs), out_shape=(jax.ShapeDty...  174 us

profile of v1, /device:TPU:1, one launch (start us, length us, event | category | flops | bytes accessed | tf_op | source)
XLA Modules:
  0.0 175.1 jit_solution(14189287604616563753)
XLA Ops:
  0.0 173.6 %diffusion.1 = (f32[32,512]{1,0:T(8,128)}, bf16[20,512,2048]{2,1,0:T(8,128)(2,1)}, f8e4m3fn[20,512,2048]{2,1,0:T(8,128)(4,1)}) custom-call(f32[64,512]{1,0:T(8,128)} %refs_0_.1, f32[32,512]{1,0:T(8,128)} %refs_1_.1), custom_call_target="tpu_custom_call" | custom-call | tf_op jit(solution)/shard_map/diffusion/pallas_call | solution.py:412
  173.6 1.5 copy.4

commit v2 on v1

v2 whole, which is shorter than its diff:
```python
import math

import jax
import jax.numpy as jnp
from jax import lax
from jax.experimental import pallas as pl
from jax.experimental.pallas import tpu as pltpu
from jax.sharding import PartitionSpec as P

MESH = pl.DeviceIdType.MESH
BF = jnp.bfloat16
F8 = jnp.float8_e4m3fn
F32 = jnp.float32
SHIFT = 17
STAGES = 6
KEPT = (2, 4, 6)
SENT = (0, 1, 3, 5, 7)


def features(points, stationary):
    scaled = points * math.sqrt(math.log2(math.e) / 16.0 * (64.0 / points.shape[0]))
    high = scaled.astype(BF)
    low = (scaled - high.astype(F32)).astype(BF)
    half = 0.5 * jnp.sum(scaled * scaled, axis=0, keepdims=True)
    half = SHIFT - half if stationary else half
    one = half.astype(BF).astype(F32)
    two = (half - one).astype(BF).astype(F32)
    three = half - one - two
    row = lax.broadcasted_iota(jnp.int32, (16, points.shape[1]), 0)
    unit = jnp.ones_like(one)
    if stationary:
        first, rest, middle = (one, two, three), (-unit, -unit, -unit), (high, high, low)
    else:
        first, rest, middle = (unit, unit, unit), (one, two, three), (high, low, high)
    extra = jnp.zeros((16, points.shape[1]), F32)
    for index, value in enumerate(first + rest):
        extra = jnp.where(row == index, value, extra)
    pad = jnp.zeros((48, points.shape[1]), BF)
    return jnp.concatenate(middle + (extra.astype(BF), pad), axis=0)


def inverse_factor(gram):
    n = gram.shape[0]
    row = lax.broadcasted_iota(jnp.int32, (n, n), 0)
    column = lax.broadcasted_iota(jnp.int32, (n, n), 1)
    inverse = jnp.where(row == column, 1.0, 0.0).astype(F32)
    for c in range(n):
        pivot = gram[c : c + 1, c : c + 1]
        root = lax.rsqrt(pivot)
        root = root * (1.5 - 0.5 * pivot * root * root)
        line = gram[c : c + 1, :] * root
        line_inverse = inverse[c : c + 1, :] * root
        factor = jnp.where(row[:, :1] > c, gram[:, c : c + 1] * root, 0.0)
        gram = jnp.where(row == c, line, gram - factor * line)
        inverse = jnp.where(row == c, line_inverse, inverse - factor * line_inverse)
    return inverse


def kernel(
    X, Z, frames, start, out, far_high, far_low,
    near_high, near_low, stage_high, stage_low, zframes, fall, sall, gall, iall, stat, turned,
    acc, low_acc, dacc, part, line_part, dgot, line_got, got_one, got_two, degree, gram_all, gram_col,
    f_recv, s_recv, g_recv, zf_recv, d_recv, line_recv, i_recv, one_recv, two_recv, p_recv, q_recv,
    send, forward, write_sem, read_sem,
):
    NO = X * X
    NB = 2 * NO
    B = frames.shape[1]
    R = Z * B
    V = start.shape[0]
    NH = len(SENT) * (NB // 8)
    total = X * X * 2 * Z * B
    me, z = lax.axis_index("row"), lax.axis_index("col")
    core, chip = lax.rem(me, 2), me // 2
    cx, cy = chip // X, lax.rem(chip, X)

    rows_x = [lax.rem(cx + d, X) * (2 * X) + core for d in range(X)]
    rows_y = [lax.rem(cy + d, X) * 2 for d in range(X)]

    def plane(o):
        return {"row": rows_x[(X - o // X) % X] + rows_y[(X - o % X) % X], "col": z}

    sibling = {"row": chip * 2 + 1 - core, "col": z}

    cols = [lax.rem(z + d, Z) for d in range(Z)]

    def along(dz):
        return {"row": me, "col": cols[dz]}

    def post(d):
        return {"row": me if d < Z else chip * 2 + 1 - core, "col": cols[(Z - d % Z) % Z]}

    def push(src, dst, send_sem, recv_sem, device):
        pltpu.make_async_remote_copy(
            src_ref=src, dst_ref=dst, send_sem=send_sem, recv_sem=recv_sem, device_id=device, device_id_type=MESH
        ).start()

    def arrived(ref, sem):
        pltpu.make_async_remote_copy(
            src_ref=ref, dst_ref=ref, send_sem=send.at[0], recv_sem=sem, device_id=sibling, device_id_type=MESH
        ).wait_recv()

    def left(ref, sem):
        pltpu.make_async_remote_copy(
            src_ref=ref, dst_ref=ref, send_sem=sem, recv_sem=f_recv.at[0], device_id=sibling, device_id_type=MESH
        ).wait_send()

    def gather_start(mine, buffer, recv, sem, forward_sem):
        push(mine, buffer.at[1], forward_sem, recv.at[1], sibling)
        for o in range(1, NO):
            push(mine, buffer.at[2 * o], sem, recv.at[2 * o], plane(o))

    def pass_on(o, buffer, recv, forward_sem):
        arrived(buffer.at[2 * o], recv.at[2 * o])
        push(buffer.at[2 * o], buffer.at[2 * o + 1], forward_sem, recv.at[2 * o + 1], sibling)

    def gather_end(buffer, sem, forward_sem):
        left(buffer.at[pl.ds(0, NO - 1)], sem)
        left(buffer.at[pl.ds(0, NO)], forward_sem)

    barrier = pltpu.get_barrier_semaphore()

    for o in range(1, NO):
        pl.semaphore_signal(barrier, inc=1, device_id=plane(o), device_id_type=MESH)
    for d in range(1, 2 * Z):
        pl.semaphore_signal(barrier, inc=1, device_id=post(d), device_id_type=MESH)
    pl.semaphore_wait(barrier, NO - 1 + 2 * Z - 1)

    for dz in range(1, Z):
        push(frames, zframes.at[Z - dz], send.at[1], zf_recv.at[Z - dz], along(dz))
    gather_start(frames, fall, f_recv, send.at[0], forward.at[0])
    gather_start(start, sall, s_recv, send.at[2], forward.at[1])
    fall[0] = frames[...]
    sall[0] = start[...]
    dacc[...] = jnp.zeros_like(dacc)
    stat[:, 0:B] = features(frames[...], True)
    for dz in range(1, Z):
        arrived(zframes.at[dz], zf_recv.at[dz])
        stat[:, dz * B : (dz + 1) * B] = features(zframes[dz], True)

    def writes(h, half):
        slot = lax.rem(2 * h + half, STAGES)
        return (
            pltpu.make_async_copy(stage_high.at[slot], far_high.at[half * NH + h], write_sem.at[slot, 0]),
            pltpu.make_async_copy(stage_low.at[slot], far_low.at[half * NH + h], write_sem.at[slot, 1]),
        )

    def reads(t):
        slot = lax.rem(t, STAGES)
        at = lax.rem(t + NH, 2 * NH)
        return (
            pltpu.make_async_copy(far_high.at[at], stage_high.at[slot], read_sem.at[slot, 0]),
            pltpu.make_async_copy(far_low.at[at], stage_low.at[slot], read_sem.at[slot, 1]),
        )

    HALF = R // 2
    width = min(512, HALF)

    def build(n, pieces):
        turned[...] = features(fall[n], False).T
        for half, (high_ref, low_ref) in enumerate(pieces):
            for c in range(HALF // width):
                at = slice(c * width, (c + 1) * width)
                whole = slice(half * HALF + c * width, half * HALF + (c + 1) * width)
                power = jnp.dot(turned[...], stat[:, whole], preferred_element_type=F32)
                value = jnp.exp2(power)
                high = value.astype(BF)
                high_ref[:, at] = high
                low_ref[:, at] = (value - high.astype(F32)).astype(F8)
                dacc[:, whole] += jnp.sum(value.reshape(B // 8, 8, width), axis=0)

    def build_group(g, _):
        for i in range(8):
            n = g * 8 + i
            if i % 2 == 0:
                o = g * 4 + i // 2

                @pl.when(o + 1 < NO)
                def _():
                    pass_on(o + 1, fall, f_recv, forward.at[0])
            else:
                arrived(fall.at[n], f_recv.at[n])
            if i in KEPT:
                at = g * len(KEPT) + KEPT.index(i)
                build(n, [(near_high.at[half, at], near_low.at[half, at]) for half in (0, 1)])
            else:
                h = g * len(SENT) + SENT.index(i)

                @pl.when(h >= STAGES // 2)
                def _():
                    for copy in writes(h - STAGES // 2, 0) + writes(h - STAGES // 2, 1):
                        copy.wait()

                slots = [lax.rem(2 * h + half, STAGES) for half in (0, 1)]
                build(n, [(stage_high.at[slot], stage_low.at[slot]) for slot in slots])
                for copy in writes(h, 0) + writes(h, 1):
                    copy.start()
        return 0

    lax.fori_loop(0, NB // 8, build_group, 0)

    for dz in range(Z):
        line_part[dz] = jnp.sum(dacc[:, dz * B : (dz + 1) * B], axis=0, keepdims=True)
    for dz in range(1, Z):
        push(line_part.at[dz], dgot.at[Z - dz], send.at[3], d_recv.at[Z - dz], along(dz))
    for h in range(NH - STAGES // 2, NH):
        for copy in writes(h, 0) + writes(h, 1):
            copy.wait()
    for t in range(STAGES):
        for copy in reads(t):
            copy.start()
    density = line_part[0]
    for dz in range(1, Z):
        arrived(dgot.at[dz], d_recv.at[dz])
        density = density + dgot[dz]
    iall[0] = 1.0 / (density * 2.0**-SHIFT)
    push(iall.at[0], iall.at[1], forward.at[2], i_recv.at[0], sibling)
    for o in range(1, NO):
        pass_on(o, sall, s_recv, forward.at[1])
    arrived(iall.at[1], i_recv.at[0])
    for o in range(1, NO):
        push(iall.at[pl.ds(0, 2)], iall.at[pl.ds(2 * o, 2)], send.at[4], i_recv.at[o], plane(o))
    acc[...] = jnp.zeros_like(acc)
    low_acc[...] = jnp.zeros_like(low_acc)
    gather_end(fall, send.at[0], forward.at[0])
    gather_end(sall, send.at[2], forward.at[1])
    left(zframes.at[pl.ds(0, Z - 1)], send.at[1])
    left(dgot.at[pl.ds(0, Z - 1)], send.at[3])
    for o in range(1, NO):
        arrived(iall.at[pl.ds(2 * o, 2)], i_recv.at[o])
    largest = jnp.max(jnp.max(iall[...], axis=0), axis=1, keepdims=True)
    low_weight = 400.0 / (6.0 * largest)

    def sweep(n, half, vectors, with_degree, high_ref, low_ref):
        inverse = iall[n]
        weights = vectors[n] * inverse
        high = weights.astype(BF)
        low = (weights - high.astype(F32)).astype(BF)
        rows = 2 * V
        pieces = [high, low]
        if with_degree:
            inverse_high = inverse.astype(BF).astype(F32)
            row = lax.broadcasted_iota(jnp.int32, (16, B), 0)
            pieces += [jnp.where(row < 8, inverse_high, inverse - inverse_high).astype(BF)]
            rows += 16
        spread = jnp.concatenate(pieces, axis=0)
        at = slice(half * HALF, (half + 1) * HALF)
        acc[0:rows, at] += jnp.dot(spread, high_ref[...], preferred_element_type=F32)
        low_acc[:, at] += jnp.dot((weights * low_weight).astype(F8), low_ref[...], preferred_element_type=F32)

    def sweep_half(half, vectors, recv, with_degree, passing, extra):
        early = half == 1

        def group(g, _):
            extra(g)
            for i in range(8):
                n = g * 8 + i
                if early and i % 2 == 1:
                    arrived(vectors.at[n], recv.at[n])
                elif early and passing:
                    o = g * 4 + i // 2

                    @pl.when(o + 1 < NO)
                    def _():
                        pass_on(o + 1, vectors, recv, forward.at[3])

                if i in KEPT:
                    at = g * len(KEPT) + KEPT.index(i)
                    sweep(n, half, vectors, with_degree, near_high.at[half, at], near_low.at[half, at])
                else:
                    t = (0 if early else NH) + g * len(SENT) + SENT.index(i)
                    for copy in reads(t):
                        copy.wait()
                    slot = lax.rem(t, STAGES)
                    sweep(n, half, vectors, with_degree, stage_high.at[slot], stage_low.at[slot])

                    @pl.when(t + STAGES < 2 * NH)
                    def _():
                        for copy in reads(t + STAGES):
                            copy.start()

            return 0

        lax.fori_loop(0, NB // 8, group, 0)

    def own_sum(half, got, recv, sem, with_degree):
        for dz in reversed(range(half * Z // 2, (half + 1) * Z // 2)):
            at = slice(dz * B, (dz + 1) * B)
            part[dz] = (acc[0:V, at] + acc[V : 2 * V, at]) * 2.0**-SHIFT + low_acc[:, at] * (
                2.0**-SHIFT / low_weight
            )
            if dz:
                push(part.at[dz], got.at[Z - dz], sem, recv.at[Z - dz], along(dz))
            if with_degree:
                line_part[dz] = (acc[2 * V : 2 * V + 1, at] + acc[2 * V + 8 : 2 * V + 9, at]) * 2.0**-SHIFT
                if dz:
                    push(line_part.at[dz], line_got.at[Z - dz], send.at[3], line_recv.at[Z - dz], along(dz))

    def own_total(source, got, recv):
        result = source[0]
        for dz in range(1, Z):
            arrived(got.at[dz], recv.at[dz])
            result = result + got[dz]
        return result

    def sweep_all(vectors, got, recv, v_recv, sem, with_degree, passing, extra):
        for half in (1, 0):
            sweep_half(half, vectors, v_recv, with_degree, passing, extra if half == 0 else lambda g: None)
            own_sum(half, got, recv, sem, with_degree)

    def gram_of(vectors):
        return lax.dot_general(
            vectors, vectors, (((1,), (1,)), ((), ())), precision=lax.Precision.HIGHEST, preferred_element_type=F32
        ) * (1.0 / total)

    def gram_send(which, vectors):
        gram_all[which, 0] = gram_of(vectors)
        for o in range(1, NO):
            push(gram_all.at[which, 0], gram_all.at[which, o], send.at[5 + which], p_recv.at[which, o], plane(o))

    def gram_turn(which):
        for o in range(1, NO):
            arrived(gram_all.at[which, o], p_recv.at[which, o])
        gram_col[which, 0] = jnp.sum(gram_all[which], axis=0)
        for d in range(1, 2 * Z):
            push(gram_col.at[which, 0], gram_col.at[which, d], send.at[7 + which], q_recv.at[which, d], post(d))

    def gram_total(which):
        for d in range(1, 2 * Z):
            arrived(gram_col.at[which, d], q_recv.at[which, d])
        return jnp.sum(gram_col[which], axis=0)

    def gram_end(which):
        left(gram_all.at[which, pl.ds(0, NO - 1)], send.at[5 + which])
        left(gram_col.at[which, pl.ds(0, 2 * Z - 1)], send.at[7 + which])

    sweep_all(sall, got_one, one_recv, s_recv, send.at[9], True, False, lambda g: None)
    for t in range(STAGES):
        for copy in reads(t):
            copy.start()
    acc[...] = jnp.zeros_like(acc)
    low_acc[...] = jnp.zeros_like(low_acc)
    left(iall.at[0], forward.at[2])
    left(iall.at[pl.ds(0, 2 * (NO - 1))], send.at[4])
    grown = own_total(part, got_one, one_recv)
    degree[...] = own_total(line_part, line_got, line_recv)
    grown = grown / degree[...]
    gall[0] = grown
    gather_start(gall.at[0], gall, g_recv, send.at[10], forward.at[3])
    gram_send(0, grown)
    left(part.at[pl.ds(0, Z - 1)], send.at[9])
    left(line_part.at[pl.ds(0, Z - 1)], send.at[3])

    def turn_first(g):
        @pl.when(g == NB // 8 - 1)
        def _():
            gram_turn(0)

    sweep_all(gall, got_two, two_recv, g_recv, send.at[11], False, True, turn_first)
    first = inverse_factor(gram_total(0))
    grown_two = own_total(part, got_two, two_recv) / degree[...]
    grown_two = jnp.dot(first, grown_two, precision=lax.Precision.HIGHEST, preferred_element_type=F32)
    gram_send(1, grown_two)
    gather_end(gall, send.at[10], forward.at[3])
    left(part.at[pl.ds(0, Z - 1)], send.at[11])
    gram_end(0)
    gram_turn(1)
    second = inverse_factor(gram_total(1))
    out[...] = jnp.dot(second, grown_two, precision=lax.Precision.HIGHEST, preferred_element_type=F32)
    gram_end(1)


def solution(mesh):
    X = math.isqrt(mesh.shape["row"] // 2)
    Z = mesh.shape["col"]
    NO, NB = X * X, 2 * X * X

    def step(frames, start):
        F, B = frames.shape
        V = start.shape[0]
        R = Z * B
        near, far = len(KEPT) * (NB // 8), len(SENT) * (NB // 8)
        vmem = pl.BlockSpec(memory_space=pltpu.VMEM)
        hbm = pl.BlockSpec(memory_space=pltpu.HBM)
        dma = pltpu.SemaphoreType.DMA
        basis, _, _ = pl.pallas_call(
            lambda *refs: kernel(X, Z, *refs),
            out_shape=(
                jax.ShapeDtypeStruct((V, B), F32),
                jax.ShapeDtypeStruct((2 * far, B, R // 2), BF),
                jax.ShapeDtypeStruct((2 * far, B, R // 2), F8),
            ),
            in_specs=[vmem, vmem],
            out_specs=(vmem, hbm, hbm),
            scratch_shapes=[
                pltpu.VMEM((2, near, B, R // 2), BF),
                pltpu.VMEM((2, near, B, R // 2), F8),
                pltpu.VMEM((STAGES, B, R // 2), BF),
                pltpu.VMEM((STAGES, B, R // 2), F8),
                pltpu.VMEM((Z, F, B), F32),
                pltpu.VMEM((NB, F, B), F32),
                pltpu.VMEM((NB, V, B), F32),
                pltpu.VMEM((NB, V, B), F32),
                pltpu.VMEM((NB, 1, B), F32),
                pltpu.VMEM((256, R), BF),
                pltpu.VMEM((B, 256), BF),
                pltpu.VMEM((2 * V + 16, R), F32),
                pltpu.VMEM((V, R), F32),
                pltpu.VMEM((8, R), F32),
                pltpu.VMEM((Z, V, B), F32),
                pltpu.VMEM((Z, 1, B), F32),
                pltpu.VMEM((Z, 1, B), F32),
                pltpu.VMEM((Z, 1, B), F32),
                pltpu.VMEM((Z, V, B), F32),
                pltpu.VMEM((Z, V, B), F32),
                pltpu.VMEM((1, B), F32),
                pltpu.VMEM((2, NO, V, V), F32),
                pltpu.VMEM((2, 2 * Z, V, V), F32),
                dma((NB,)), dma((NB,)), dma((NB,)),
                dma((Z,)), dma((Z,)), dma((Z,)), dma((NO,)), dma((Z,)), dma((Z,)),
                dma((2, NO)), dma((2, 2 * Z)),
                dma((12,)), dma((4,)), dma((STAGES, 2)), dma((STAGES, 2)),
            ],
            compiler_params=pltpu.CompilerParams(
                collective_id=0, has_side_effects=True, vmem_limit_bytes=64 * 1024 * 1024 - 512 * 1024
            ),
            name="diffusion",
        )(frames, start)
        return basis

    return jax.shard_map(
        step,
        mesh=mesh,
        in_specs=(P(None, ("row", "col")), P(None, ("row", "col"))),
        out_specs=P(None, ("row", "col")),
        check_vma=False,
    )
```

time: 175 us -> 162 us (0.926)
  Pallas kernels: 174 us -> 161 us
    pallas_call x1, Pallas kernels: 174 us -> 161 us  [step(): pl.pallas_call(lambda *refs: kernel(X, Z, *refs), out_shape=(jax.ShapeDty...]
where the time goes in v2:
time: 162 us
  Pallas kernels  161 us (99%)
    pallas_call x1, Pallas kernels, step(): pl.pallas_call(lambda *refs: kernel(X, Z, *refs), out_shape=(jax.ShapeDty...  161 us

profile of v2, /device:TPU:1, one launch (start us, length us, event | category | flops | bytes accessed | tf_op | source)
XLA Modules:
  0.0 162.2 jit_solution(11101169059654392466)
XLA Ops:
  0.0 160.8 %diffusion.1 = (f32[32,512]{1,0:T(8,128)}, bf16[40,512,1024]{2,1,0:T(8,128)(2,1)}, f8e4m3fn[40,512,1024]{2,1,0:T(8,128)(4,1)}) custom-call(f32[64,512]{1,0:T(8,128)} %refs_0_.1, f32[32,512]{1,0:T(8,128)} %refs_1_.1), custom_call_target="tpu_custom_call" | custom-call | tf_op jit(solution)/shard_map/diffusion/pallas_call | solution.py:386
  160.8 1.5 copy.4

commit v3 on v2

--- a/solution.py
+++ b/solution.py
@@ -12,7 +12,9 @@
 F8 = jnp.float8_e4m3fn
 F32 = jnp.float32
 SHIFT = 17
-STAGES = 6
+BLOCKS = 3
+FRAMES_AHEAD = 6
+GROWN_AHEAD = 8
 KEPT = (2, 4, 6)
 SENT = (0, 1, 3, 5, 7)
 
@@ -56,6 +58,15 @@
     return inverse
 
 
+def chip_order(X):
+    hops = [min(d, X - d) for d in range(X)]
+
+    def key(place):
+        return max(hops[place[0]], hops[place[1]]), hops[place[0]] + hops[place[1]], sum(place), place
+
+    return sorted(((dx, dy) for dx in range(X) for dy in range(X)), key=key)
+
+
 def kernel(
     X, Z, frames, start, out, far_high, far_low,
     near_high, near_low, stage_high, stage_low, zframes, fall, sall, gall, iall, stat, turned,
@@ -77,8 +88,11 @@
     rows_x = [lax.rem(cx + d, X) * (2 * X) + core for d in range(X)]
     rows_y = [lax.rem(cy + d, X) * 2 for d in range(X)]
 
+    places = chip_order(X)
+
     def plane(o):
-        return {"row": rows_x[(X - o // X) % X] + rows_y[(X - o % X) % X], "col": z}
+        dx, dy = places[o]
+        return {"row": rows_x[(X - dx) % X] + rows_y[(X - dy) % X], "col": z}
 
     sibling = {"row": chip * 2 + 1 - core, "col": z}
 
@@ -105,10 +119,21 @@
             src_ref=ref, dst_ref=ref, send_sem=sem, recv_sem=f_recv.at[0], device_id=sibling, device_id_type=MESH
         ).wait_send()
 
-    def gather_start(mine, buffer, recv, sem, forward_sem):
+    def gather_send(o, mine, buffer, recv, sem):
+        if 0 < o < NO:
+            push(mine, buffer.at[2 * o], sem, recv.at[2 * o], plane(o))
+
+    def gather_start(ahead, mine, buffer, recv, sem, forward_sem):
         push(mine, buffer.at[1], forward_sem, recv.at[1], sibling)
-        for o in range(1, NO):
-            push(mine, buffer.at[2 * o], sem, recv.at[2 * o], plane(o))
+        for o in range(1, ahead):
+            gather_send(o, mine, buffer, recv, sem)
+
+    def beside(g, step, send_some):
+        for known in range(NB // 8):
+
+            @pl.when(g == known)
+            def _(known=known):
+                send_some(known * 4 + step)
 
     def pass_on(o, buffer, recv, forward_sem):
         arrived(buffer.at[2 * o], recv.at[2 * o])
@@ -128,8 +153,8 @@
 
     for dz in range(1, Z):
         push(frames, zframes.at[Z - dz], send.at[1], zf_recv.at[Z - dz], along(dz))
-    gather_start(frames, fall, f_recv, send.at[0], forward.at[0])
-    gather_start(start, sall, s_recv, send.at[2], forward.at[1])
+    gather_start(FRAMES_AHEAD, frames, fall, f_recv, send.at[0], forward.at[0])
+    gather_start(0, start, sall, s_recv, send.at[2], forward.at[1])
     fall[0] = frames[...]
     sall[0] = start[...]
     dacc[...] = jnp.zeros_like(dacc)
@@ -138,41 +163,58 @@
         arrived(zframes.at[dz], zf_recv.at[dz])
         stat[:, dz * B : (dz + 1) * B] = features(zframes[dz], True)
 
-    def writes(h, half):
-        slot = lax.rem(2 * h + half, STAGES)
-        return (
-            pltpu.make_async_copy(stage_high.at[slot], far_high.at[half * NH + h], write_sem.at[slot, 0]),
-            pltpu.make_async_copy(stage_low.at[slot], far_low.at[half * NH + h], write_sem.at[slot, 1]),
-        )
-
-    def reads(t):
+    STAGES = BLOCKS * Z
+
+    def writes(h):
+        copies = []
+        for dz in range(Z):
+            slot = lax.rem(Z * h + dz, STAGES)
+            copies += [
+                pltpu.make_async_copy(stage_high.at[slot], far_high.at[dz * NH + h], write_sem.at[slot, 0]),
+                pltpu.make_async_copy(stage_low.at[slot], far_low.at[dz * NH + h], write_sem.at[slot, 1]),
+            ]
+        return copies
+
+    def reads(t, at):
         slot = lax.rem(t, STAGES)
-        at = lax.rem(t + NH, 2 * NH)
         return (
             pltpu.make_async_copy(far_high.at[at], stage_high.at[slot], read_sem.at[slot, 0]),
             pltpu.make_async_copy(far_low.at[at], stage_low.at[slot], read_sem.at[slot, 1]),
         )
 
-    HALF = R // 2
-    width = min(512, HALF)
+    def read_start(t):
+        @pl.when(t < (Z - 1) * NH)
+        def _():
+            for copy in reads(t, (1 + lax.rem(t, Z - 1)) * NH + t // (Z - 1)):
+                copy.start()
+
+        @pl.when((t >= (Z - 1) * NH) & (t < Z * NH))
+        def _():
+            for copy in reads(t, t - (Z - 1) * NH):
+                copy.start()
 
     def build(n, pieces):
         turned[...] = features(fall[n], False).T
-        for half, (high_ref, low_ref) in enumerate(pieces):
-            for c in range(HALF // width):
-                at = slice(c * width, (c + 1) * width)
-                whole = slice(half * HALF + c * width, half * HALF + (c + 1) * width)
-                power = jnp.dot(turned[...], stat[:, whole], preferred_element_type=F32)
-                value = jnp.exp2(power)
-                high = value.astype(BF)
-                high_ref[:, at] = high
-                low_ref[:, at] = (value - high.astype(F32)).astype(F8)
-                dacc[:, whole] += jnp.sum(value.reshape(B // 8, 8, width), axis=0)
+        for dz, (high_ref, low_ref) in enumerate(pieces):
+            at = slice(dz * B, (dz + 1) * B)
+            power = jnp.dot(turned[...], stat[:, at], preferred_element_type=F32)
+            value = jnp.exp2(power)
+            high = value.astype(BF)
+            high_ref[...] = high
+            low_ref[...] = (value - high.astype(F32)).astype(F8)
+            dacc[:, at] += jnp.sum(value.reshape(B // 8, 8, B), axis=0)
+
+    def send_inputs(o):
+        gather_send(o + FRAMES_AHEAD, frames, fall, f_recv, send.at[0])
+        later = 2 * (o - NO // 2)
+        gather_send(later + 1, start, sall, s_recv, send.at[2])
+        gather_send(later + 2, start, sall, s_recv, send.at[2])
 
     def build_group(g, _):
         for i in range(8):
             n = g * 8 + i
             if i % 2 == 0:
+                beside(g, i // 2, send_inputs)
                 o = g * 4 + i // 2
 
                 @pl.when(o + 1 < NO)
@@ -182,18 +224,18 @@
                 arrived(fall.at[n], f_recv.at[n])
             if i in KEPT:
                 at = g * len(KEPT) + KEPT.index(i)
-                build(n, [(near_high.at[half, at], near_low.at[half, at]) for half in (0, 1)])
+                build(n, [(near_high.at[dz, at], near_low.at[dz, at]) for dz in range(Z)])
             else:
                 h = g * len(SENT) + SENT.index(i)
 
-                @pl.when(h >= STAGES // 2)
+                @pl.when(h >= BLOCKS)
                 def _():
-                    for copy in writes(h - STAGES // 2, 0) + writes(h - STAGES // 2, 1):
+                    for copy in writes(h - BLOCKS):
                         copy.wait()
 
-                slots = [lax.rem(2 * h + half, STAGES) for half in (0, 1)]
+                slots = [lax.rem(Z * h + dz, STAGES) for dz in range(Z)]
                 build(n, [(stage_high.at[slot], stage_low.at[slot]) for slot in slots])
-                for copy in writes(h, 0) + writes(h, 1):
+                for copy in writes(h):
                     copy.start()
         return 0
 
@@ -201,23 +243,26 @@
 
     for dz in range(Z):
         line_part[dz] = jnp.sum(dacc[:, dz * B : (dz + 1) * B], axis=0, keepdims=True)
-    for dz in range(1, Z):
-        push(line_part.at[dz], dgot.at[Z - dz], send.at[3], d_recv.at[Z - dz], along(dz))
-    for h in range(NH - STAGES // 2, NH):
-        for copy in writes(h, 0) + writes(h, 1):
+    for dz in range(Z):
+        for other in range(2):
+            if dz or other:
+                place = {"row": sibling["row"] if other else me, "col": cols[dz]}
+                slot = (Z - dz) % Z
+                push(line_part.at[dz], dgot.at[other, slot], send.at[3], d_recv.at[other, slot], place)
+    for h in range(NH - BLOCKS, NH):
+        for copy in writes(h):
             copy.wait()
     for t in range(STAGES):
-        for copy in reads(t):
-            copy.start()
-    density = line_part[0]
-    for dz in range(1, Z):
-        arrived(dgot.at[dz], d_recv.at[dz])
-        density = density + dgot[dz]
-    iall[0] = 1.0 / (density * 2.0**-SHIFT)
-    push(iall.at[0], iall.at[1], forward.at[2], i_recv.at[0], sibling)
+        read_start(t)
     for o in range(1, NO):
         pass_on(o, sall, s_recv, forward.at[1])
-    arrived(iall.at[1], i_recv.at[0])
+    dgot[0, 0] = line_part[0]
+    for other in range(2):
+        for dz in range(Z):
+            if dz or other:
+                arrived(dgot.at[other, dz], d_recv.at[other, dz])
+        density = sum(dgot[other, dz] for dz in range(Z))
+        iall[other] = 1.0 / (density * 2.0**-SHIFT)
     for o in range(1, NO):
         push(iall.at[pl.ds(0, 2)], iall.at[pl.ds(2 * o, 2)], send.at[4], i_recv.at[o], plane(o))
     acc[...] = jnp.zeros_like(acc)
@@ -225,40 +270,44 @@
     gather_end(fall, send.at[0], forward.at[0])
     gather_end(sall, send.at[2], forward.at[1])
     left(zframes.at[pl.ds(0, Z - 1)], send.at[1])
-    left(dgot.at[pl.ds(0, Z - 1)], send.at[3])
+    left(iall.at[pl.ds(0, 2 * Z - 1)], send.at[3])
     for o in range(1, NO):
         arrived(iall.at[pl.ds(2 * o, 2)], i_recv.at[o])
     largest = jnp.max(jnp.max(iall[...], axis=0), axis=1, keepdims=True)
     low_weight = 400.0 / (6.0 * largest)
 
-    def sweep(n, half, vectors, with_degree, high_ref, low_ref):
+    def sweep(n, vectors, with_degree, pieces):
         inverse = iall[n]
         weights = vectors[n] * inverse
         high = weights.astype(BF)
         low = (weights - high.astype(F32)).astype(BF)
         rows = 2 * V
-        pieces = [high, low]
+        spread = [high, low]
         if with_degree:
             inverse_high = inverse.astype(BF).astype(F32)
             row = lax.broadcasted_iota(jnp.int32, (16, B), 0)
-            pieces += [jnp.where(row < 8, inverse_high, inverse - inverse_high).astype(BF)]
+            spread += [jnp.where(row < 8, inverse_high, inverse - inverse_high).astype(BF)]
             rows += 16
-        spread = jnp.concatenate(pieces, axis=0)
-        at = slice(half * HALF, (half + 1) * HALF)
-        acc[0:rows, at] += jnp.dot(spread, high_ref[...], preferred_element_type=F32)
-        low_acc[:, at] += jnp.dot((weights * low_weight).astype(F8), low_ref[...], preferred_element_type=F32)
-
-    def sweep_half(half, vectors, recv, with_degree, passing, extra):
-        early = half == 1
-
+        spread = jnp.concatenate(spread, axis=0)
+        coarse = (weights * low_weight).astype(F8)
+        for dz, high_ref, low_ref in pieces:
+            at = slice(dz * B, (dz + 1) * B)
+            acc[0:rows, at] += jnp.dot(spread, high_ref[...], preferred_element_type=F32)
+            low_acc[:, at] += jnp.dot(coarse, low_ref[...], preferred_element_type=F32)
+
+    def send_grown(o):
+        gather_send(o + GROWN_AHEAD, gall.at[0], gall, g_recv, send.at[10])
+
+    def sweep_part(first, pieces, vectors, recv, with_degree, passing, extra):
         def group(g, _):
             extra(g)
             for i in range(8):
                 n = g * 8 + i
-                if early and i % 2 == 1:
+                if first and i % 2 == 1:
                     arrived(vectors.at[n], recv.at[n])
-                elif early and passing:
+                elif first and passing:
                     o = g * 4 + i // 2
+                    beside(g, i // 2, send_grown)
 
                     @pl.when(o + 1 < NO)
                     def _():
@@ -266,35 +315,33 @@
 
                 if i in KEPT:
                     at = g * len(KEPT) + KEPT.index(i)
-                    sweep(n, half, vectors, with_degree, near_high.at[half, at], near_low.at[half, at])
+                    sweep(n, vectors, with_degree, [(dz, near_high.at[dz, at], near_low.at[dz, at]) for dz in pieces])
                 else:
-                    t = (0 if early else NH) + g * len(SENT) + SENT.index(i)
-                    for copy in reads(t):
-                        copy.wait()
-                    slot = lax.rem(t, STAGES)
-                    sweep(n, half, vectors, with_degree, stage_high.at[slot], stage_low.at[slot])
-
-                    @pl.when(t + STAGES < 2 * NH)
-                    def _():
-                        for copy in reads(t + STAGES):
-                            copy.start()
+                    h = g * len(SENT) + SENT.index(i)
+                    times = [(Z - 1) * h + k if first else (Z - 1) * NH + h for k in range(len(pieces))]
+                    taken = []
+                    for t, dz in zip(times, pieces):
+                        for copy in reads(t, dz * NH + h):
+                            copy.wait()
+                        slot = lax.rem(t, STAGES)
+                        taken.append((dz, stage_high.at[slot], stage_low.at[slot]))
+                    sweep(n, vectors, with_degree, taken)
+                    for t in times:
+                        read_start(t + STAGES)
 
             return 0
 
         lax.fori_loop(0, NB // 8, group, 0)
 
-    def own_sum(half, got, recv, sem, with_degree):
-        for dz in reversed(range(half * Z // 2, (half + 1) * Z // 2)):
-            at = slice(dz * B, (dz + 1) * B)
-            part[dz] = (acc[0:V, at] + acc[V : 2 * V, at]) * 2.0**-SHIFT + low_acc[:, at] * (
-                2.0**-SHIFT / low_weight
-            )
+    def own_sum(dz, got, recv, sem, with_degree):
+        at = slice(dz * B, (dz + 1) * B)
+        part[dz] = (acc[0:V, at] + acc[V : 2 * V, at]) * 2.0**-SHIFT + low_acc[:, at] * (2.0**-SHIFT / low_weight)
+        if dz:
+            push(part.at[dz], got.at[Z - dz], sem, recv.at[Z - dz], along(dz))
+        if with_degree:
+            line_part[dz] = (acc[2 * V : 2 * V + 1, at] + acc[2 * V + 8 : 2 * V + 9, at]) * 2.0**-SHIFT
             if dz:
-                push(part.at[dz], got.at[Z - dz], sem, recv.at[Z - dz], along(dz))
-            if with_degree:
-                line_part[dz] = (acc[2 * V : 2 * V + 1, at] + acc[2 * V + 8 : 2 * V + 9, at]) * 2.0**-SHIFT
-                if dz:
-                    push(line_part.at[dz], line_got.at[Z - dz], send.at[3], line_recv.at[Z - dz], along(dz))
+                push(line_part.at[dz], line_got.at[Z - dz], send.at[3], line_recv.at[Z - dz], along(dz))
 
     def own_total(source, got, recv):
         result = source[0]
@@ -304,9 +351,10 @@
         return result
 
     def sweep_all(vectors, got, recv, v_recv, sem, with_degree, passing, extra):
-        for half in (1, 0):
-            sweep_half(half, vectors, v_recv, with_degree, passing, extra if half == 0 else lambda g: None)
-            own_sum(half, got, recv, sem, with_degree)
+        for first, pieces in ((True, range(1, Z)), (False, range(1))):
+            sweep_part(first, pieces, vectors, v_recv, with_degree, passing, (lambda g: None) if first else extra)
+            for dz in pieces:
+                own_sum(dz, got, recv, sem, with_degree)
 
     def gram_of(vectors):
         return lax.dot_general(
@@ -314,7 +362,8 @@
         ) * (1.0 / total)
 
     def gram_send(which, vectors):
-        gram_all[which, 0] = gram_of(vectors)
+        gram = gram_of(vectors)
+        gram_all[which, 0] = jnp.concatenate([gram[i : i + 8] for i in range(0, V, 8)], axis=1)
         for o in range(1, NO):
             push(gram_all.at[which, 0], gram_all.at[which, o], send.at[5 + which], p_recv.at[which, o], plane(o))
 
@@ -328,7 +377,8 @@
     def gram_total(which):
         for d in range(1, 2 * Z):
             arrived(gram_col.at[which, d], q_recv.at[which, d])
-        return jnp.sum(gram_col[which], axis=0)
+        packed = jnp.sum(gram_col[which], axis=0)
+        return jnp.concatenate([packed[:, i : i + V] for i in range(0, V * (V // 8), V)], axis=0)
 
     def gram_end(which):
         left(gram_all.at[which, pl.ds(0, NO - 1)], send.at[5 + which])
@@ -336,17 +386,15 @@
 
     sweep_all(sall, got_one, one_recv, s_recv, send.at[9], True, False, lambda g: None)
     for t in range(STAGES):
-        for copy in reads(t):
-            copy.start()
+        read_start(t)
     acc[...] = jnp.zeros_like(acc)
     low_acc[...] = jnp.zeros_like(low_acc)
-    left(iall.at[0], forward.at[2])
     left(iall.at[pl.ds(0, 2 * (NO - 1))], send.at[4])
     grown = own_total(part, got_one, one_recv)
     degree[...] = own_total(line_part, line_got, line_recv)
     grown = grown / degree[...]
     gall[0] = grown
-    gather_start(gall.at[0], gall, g_recv, send.at[10], forward.at[3])
+    gather_start(GROWN_AHEAD, gall.at[0], gall, g_recv, send.at[10], forward.at[3])
     gram_send(0, grown)
     left(part.at[pl.ds(0, Z - 1)], send.at[9])
     left(line_part.at[pl.ds(0, Z - 1)], send.at[3])
@@ -387,16 +435,16 @@
             lambda *refs: kernel(X, Z, *refs),
             out_shape=(
                 jax.ShapeDtypeStruct((V, B), F32),
-                jax.ShapeDtypeStruct((2 * far, B, R // 2), BF),
-                jax.ShapeDtypeStruct((2 * far, B, R // 2), F8),
+                jax.ShapeDtypeStruct((Z * far, B, B), BF),
+                jax.ShapeDtypeStruct((Z * far, B, B), F8),
             ),
             in_specs=[vmem, vmem],
             out_specs=(vmem, hbm, hbm),
             scratch_shapes=[
-                pltpu.VMEM((2, near, B, R // 2), BF),
-                pltpu.VMEM((2, near, B, R // 2), F8),
-                pltpu.VMEM((STAGES, B, R // 2), BF),
-                pltpu.VMEM((STAGES, B, R // 2), F8),
+                pltpu.VMEM((Z, near, B, B), BF),
+                pltpu.VMEM((Z, near, B, B), F8),
+                pltpu.VMEM((BLOCKS * Z, B, B), BF),
+                pltpu.VMEM((BLOCKS * Z, B, B), F8),
                 pltpu.VMEM((Z, F, B), F32),
                 pltpu.VMEM((NB, F, B), F32),
                 pltpu.VMEM((NB, V, B), F32),
@@ -409,17 +457,17 @@
                 pltpu.VMEM((8, R), F32),
                 pltpu.VMEM((Z, V, B), F32),
                 pltpu.VMEM((Z, 1, B), F32),
-                pltpu.VMEM((Z, 1, B), F32),
+                pltpu.VMEM((2, Z, 1, B), F32),
                 pltpu.VMEM((Z, 1, B), F32),
                 pltpu.VMEM((Z, V, B), F32),
                 pltpu.VMEM((Z, V, B), F32),
                 pltpu.VMEM((1, B), F32),
-                pltpu.VMEM((2, NO, V, V), F32),
-                pltpu.VMEM((2, 2 * Z, V, V), F32),
+                pltpu.VMEM((2, NO, 8, V * V // 8), F32),
+                pltpu.VMEM((2, 2 * Z, 8, V * V // 8), F32),
                 dma((NB,)), dma((NB,)), dma((NB,)),
-                dma((Z,)), dma((Z,)), dma((Z,)), dma((NO,)), dma((Z,)), dma((Z,)),
+                dma((Z,)), dma((2, Z)), dma((Z,)), dma((NO,)), dma((Z,)), dma((Z,)),
                 dma((2, NO)), dma((2, 2 * Z)),
-                dma((12,)), dma((4,)), dma((STAGES, 2)), dma((STAGES, 2)),
+                dma((12,)), dma((4,)), dma((BLOCKS * Z, 2)), dma((BLOCKS * Z, 2)),
             ],
             compiler_params=pltpu.CompilerParams(
                 collective_id=0, has_side_effects=True, vmem_limit_bytes=64 * 1024 * 1024 - 512 * 1024

time: 162 us -> 137 us (0.85)
  Pallas kernels: 161 us -> 136 us
    pallas_call x1, Pallas kernels: 161 us -> 136 us  [step(): pl.pallas_call(lambda *refs: kernel(X, Z, *refs), out_shape=(jax.ShapeDty...]
where the time goes in v3:
time: 137 us
  Pallas kernels  136 us (99%)
  local copies, waits for them, and re-layouts  1.47 us (1%)
    pallas_call x1, Pallas kernels, step(): pl.pallas_call(lambda *refs: kernel(X, Z, *refs), out_shape=(jax.ShapeDty...  136 us

profile of v3, /device:TPU:1, one launch (start us, length us, event | category | flops | bytes accessed | tf_op | source)
XLA Modules:
  0.0 137.2 jit_solution(7967647506185526177)
XLA Ops:
  0.0 135.7 %diffusion.1 = (f32[32,512]{1,0:T(8,128)}, bf16[80,512,512]{2,1,0:T(8,128)(2,1)}, f8e4m3fn[80,512,512]{2,1,0:T(8,128)(4,1)}) custom-call(f32[64,512]{1,0:T(8,128)} %refs_0_.1, f32[32,512]{1,0:T(8,128)} %refs_1_.1), custom_call_target="tpu_custom_call" | custom-call | tf_op jit(solution)/shard_map/diffusion/pallas_call | solution.py:434
  135.7 1.5 %copy.4 = f32[32,512]{1,0:T(8,128)} copy(f32[32,512]{1,0:T(8,128)} %get-tuple-element.6) | data formatting | bytes 131072

commit v4 on v3

--- a/solution.py
+++ b/solution.py
@@ -13,7 +13,8 @@
 F32 = jnp.float32
 SHIFT = 17
 BLOCKS = 3
-FRAMES_AHEAD = 6
+FRAMES_AHEAD = 5
+FRAMES_RAMP = 2
 GROWN_AHEAD = 8
 KEPT = (2, 4, 6)
 SENT = (0, 1, 3, 5, 7)
@@ -149,16 +150,16 @@
         pl.semaphore_signal(barrier, inc=1, device_id=plane(o), device_id_type=MESH)
     for d in range(1, 2 * Z):
         pl.semaphore_signal(barrier, inc=1, device_id=post(d), device_id_type=MESH)
+    fall[0] = frames[...]
+    sall[0] = start[...]
+    dacc[...] = jnp.zeros_like(dacc)
+    stat[:, 0:B] = features(frames[...], True)
     pl.semaphore_wait(barrier, NO - 1 + 2 * Z - 1)
 
     for dz in range(1, Z):
         push(frames, zframes.at[Z - dz], send.at[1], zf_recv.at[Z - dz], along(dz))
     gather_start(FRAMES_AHEAD, frames, fall, f_recv, send.at[0], forward.at[0])
     gather_start(0, start, sall, s_recv, send.at[2], forward.at[1])
-    fall[0] = frames[...]
-    sall[0] = start[...]
-    dacc[...] = jnp.zeros_like(dacc)
-    stat[:, 0:B] = features(frames[...], True)
     for dz in range(1, Z):
         arrived(zframes.at[dz], zf_recv.at[dz])
         stat[:, dz * B : (dz + 1) * B] = features(zframes[dz], True)
@@ -205,7 +206,9 @@
             dacc[:, at] += jnp.sum(value.reshape(B // 8, 8, B), axis=0)
 
     def send_inputs(o):
-        gather_send(o + FRAMES_AHEAD, frames, fall, f_recv, send.at[0])
+        steps = (2 * o, 2 * o + 1) if o < FRAMES_RAMP else (o + FRAMES_RAMP,)
+        for later in steps:
+            gather_send(FRAMES_AHEAD + later, frames, fall, f_recv, send.at[0])
         later = 2 * (o - NO // 2)
         gather_send(later + 1, start, sall, s_recv, send.at[2])
         gather_send(later + 2, start, sall, s_recv, send.at[2])

time: 137 us -> 139 us (1.015)
    pallas_call x1, Pallas kernels: 136 us -> 137 us  [step(): pl.pallas_call(lambda *refs: kernel(X, Z, *refs), out_shape=(jax.ShapeDty...]
where the time goes in v4:
time: 139 us
  Pallas kernels  137 us (99%)
  local copies, waits for them, and re-layouts  1.47 us (1%)
    pallas_call x1, Pallas kernels, step(): pl.pallas_call(lambda *refs: kernel(X, Z, *refs), out_shape=(jax.ShapeDty...  137 us

profile of v4, /device:TPU:1, one launch (start us, length us, event | category | flops | bytes accessed | tf_op | source)
XLA Modules:
  0.0 138.8 jit_solution(6392118769196660527)
XLA Ops:
  0.0 137.3 %diffusion.1 = (f32[32,512]{1,0:T(8,128)}, bf16[80,512,512]{2,1,0:T(8,128)(2,1)}, f8e4m3fn[80,512,512]{2,1,0:T(8,128)(4,1)}) custom-call(f32[64,512]{1,0:T(8,128)} %refs_0_.1, f32[32,512]{1,0:T(8,128)} %refs_1_.1), custom_call_target="tpu_custom_call" | custom-call | tf_op jit(solution)/shard_map/diffusion/pallas_call | solution.py:437
  137.3 1.5 %copy.4 = f32[32,512]{1,0:T(8,128)} copy(f32[32,512]{1,0:T(8,128)} %get-tuple-element.6) | data formatting | bytes 131072
